TPU v7x, 32 devices: a whole 2x2x4 slice. The times are simulated.
32 devices in a mesh: crop: 1, res: 32 (over z, y, x, core).
Axes of the slice: x: 2, y: 2, z: 4, core: 2. Of those that a mesh axis runs over, the one named last changes fastest.
Arguments:
- homolog_symbol_ids: int32 [64, 128], P(('crop', 'res')), may hold values from 0 to 22
- residue_attend_mask: int32 [128], P('crop'), may hold values 0 or 1
- alignment_state: bfloat16 [64, 128, 256], P(('crop', 'res')), may hold values from -6 to 6
- pair: bfloat16 [128, 128, 128], P(('crop', 'res')), may hold values from -6 to 6
- symbol_lookup_matrix: bfloat16 [23, 256], replicated, may hold values from -3 to 3
- pair_bias_weight: bfloat16 [128, 8], replicated, may hold values from -0.5 to 0.5
- row_projection_weight: bfloat16 [256, 1024], replicated, may hold values from -8 to 8
- horizontal_readout_matrix: bfloat16 [256, 256], replicated, may hold values from -0.375 to 0.375
- column_projection_weight: bfloat16 [256, 1024], replicated, may hold values from -8 to 8
- vertical_readout_matrix: bfloat16 [256, 256], replicated, may hold values from -0.375 to 0.375
- product_factor_matrices: bfloat16 [256, 64], replicated, may hold values from -0.375 to 0.375
- outer_output_weight: bfloat16 [1024, 128], replicated, may hold values from -1.5 to 1.5
- triangle_input_weight: bfloat16 [128, 640], replicated, may hold values from -0.5 to 0.5
- triangle_output_weight: bfloat16 [128, 128], replicated, may hold values from -0.5 to 0.5
Outputs:
- alignment_output: bfloat16 [64, 128, 256], P('crop', 'res')
- pair_output: bfloat16 [128, 128, 128], P(('crop', 'res'))
All inputs are finite; a program needn't handle non-finite values.
Results may differ from a plain program's by a relative error of at most 0.013.
Values may be sent and summed in bfloat16 or wider, within the bound.
A program may use at most 64 MiB of HBM per device.

v0:
```python
import jax
import jax.numpy as jnp
from jax import lax
from jax.sharding import PartitionSpec as P

EPSILON = 1e-05


def layer_normalized(input_rows, axis):
    average = jnp.mean(input_rows, axis, keepdims=True)
    centred = input_rows - average
    spread = jnp.mean(centred * centred, axis, keepdims=True)
    return centred * lax.rsqrt(spread + EPSILON)


def split_proj(input_rows, weight, head_count):
    channels = weight.shape[0]
    head_size = channels // head_count
    projected = jnp.einsum("blc,ce->ble", input_rows, weight, preferred_element_type=jnp.float32)
    lead = projected.shape[:2]
    query_tensor = (
        (projected[..., :channels] * head_size ** (-0.5))
        .astype(jnp.bfloat16)
        .reshape(lead + (head_count, head_size))
    )
    key_tensor = (
        projected[..., channels : 2 * channels]
        .astype(jnp.bfloat16)
        .reshape(lead + (head_count, head_size))
    )
    value_tensor = (
        projected[..., 2 * channels : 3 * channels]
        .astype(jnp.bfloat16)
        .reshape(lead + (head_count, head_size))
    )
    gate_values = projected[..., 3 * channels :]
    return (query_tensor, key_tensor, value_tensor, gate_values)


def attention_block_fn(query_tensor, key_tensor, value_tensor, gate_values, extra_bias, out_weight):
    scores = (
        jnp.einsum("bqhd,bkhd->bhqk", query_tensor, key_tensor, preferred_element_type=jnp.float32)
        + extra_bias
    )
    row_top = jnp.max(scores, -1, keepdims=True)
    exp_scores = jnp.exp(scores - row_top)
    weights = (exp_scores / jnp.sum(exp_scores, -1, keepdims=True)).astype(jnp.bfloat16)
    mixed = jnp.einsum("bhqk,bkhd->bqhd", weights, value_tensor, preferred_element_type=jnp.float32)
    gated = (jax.nn.sigmoid(gate_values) * mixed.reshape(gate_values.shape)).astype(jnp.bfloat16)
    return jnp.einsum("bqc,ce->bqe", gated, out_weight, preferred_element_type=jnp.float32)


def shards(
    homolog_symbol_ids,
    residue_attend_mask,
    alignment_state,
    pair,
    symbol_lookup_matrix,
    pair_bias_weight,
    row_projection_weight,
    horizontal_readout_matrix,
    column_projection_weight,
    vertical_readout_matrix,
    product_factor_matrices,
    outer_output_weight,
    triangle_input_weight,
    triangle_output_weight,
):
    residue_count = lax.axis_size("res")
    sequence_total = alignment_state.shape[0] * residue_count
    res_local = pair.shape[0]
    chain_total = pair.shape[1]
    pair_chan = pair.shape[2]
    owner_chan = pair_chan // residue_count
    outer_chan = product_factor_matrices.shape[1] // 2
    head_count = pair_bias_weight.shape[1]
    token_class_count = symbol_lookup_matrix.shape[0]
    one_hot_tokens = (
        homolog_symbol_ids[:, :, None]
        == jnp.arange(token_class_count, dtype=jnp.int32)[None, None, :]
    ).astype(jnp.bfloat16)
    alignment_initial = alignment_state.astype(jnp.float32) + jnp.einsum(
        "kly,yb->klb", one_hot_tokens, symbol_lookup_matrix, preferred_element_type=jnp.float32
    )
    pair_normed = layer_normalized(pair.astype(jnp.float32), -1).astype(jnp.bfloat16)
    bias_local = jnp.einsum(
        "ijc,ch->hij", pair_normed, pair_bias_weight, preferred_element_type=jnp.float32
    ).astype(jnp.bfloat16)
    mask_bias = (residue_attend_mask.astype(jnp.float32) - 1.0) * 10000.0
    row_input = layer_normalized(alignment_initial, -1).astype(jnp.bfloat16)
    query_tensor, key_tensor, value_tensor, gate_values = split_proj(
        row_input, row_projection_weight, head_count
    )
    bias_all = lax.all_gather(bias_local, "res", axis=1, tiled=True)
    extra_bias = bias_all.astype(jnp.float32)[None] + mask_bias[None, None, None, :]
    row_attention_update = attention_block_fn(
        query_tensor, key_tensor, value_tensor, gate_values, extra_bias, horizontal_readout_matrix
    )
    alignment_after_rows = (alignment_initial + row_attention_update).astype(jnp.bfloat16)
    alignment_columns = lax.all_to_all(
        alignment_after_rows, "res", split_axis=1, concat_axis=0, tiled=True
    )
    column_start = jnp.swapaxes(alignment_columns, 0, 1).astype(jnp.float32)
    col_in = layer_normalized(column_start, -1).astype(jnp.bfloat16)
    col_queries, col_keys, col_values, col_gating = split_proj(
        col_in, column_projection_weight, head_count
    )
    alignment_after_columns = column_start + attention_block_fn(
        col_queries, col_keys, col_values, col_gating, jnp.float32(0.0), vertical_readout_matrix
    )
    alignment_output = jnp.swapaxes(alignment_after_columns, 0, 1).astype(jnp.bfloat16)
    outer_input = layer_normalized(alignment_after_columns, -1).astype(jnp.bfloat16)
    factor_ab = jnp.einsum(
        "rsc,ce->rse", outer_input, product_factor_matrices, preferred_element_type=jnp.float32
    )
    left = factor_ab[..., :outer_chan].astype(jnp.bfloat16)
    latter_factor = (
        factor_ab[..., outer_chan:]
        .astype(jnp.bfloat16)
        .reshape(res_local, sequence_total * outer_chan)
    )
    piece = lax.all_gather(latter_factor, "res", axis=0, tiled=True)
    count = piece.shape[0]
    right_rows = piece.reshape(count, sequence_total, outer_chan)
    cross_product_result = (
        jnp.einsum("isc,jsd->ijcd", left, right_rows, preferred_element_type=jnp.float32)
        / sequence_total
    ).astype(jnp.bfloat16)
    update = jnp.einsum(
        "ije,ez->ijz",
        cross_product_result.reshape(res_local, count, outer_chan * outer_chan),
        outer_output_weight,
        preferred_element_type=jnp.float32,
    )
    pair_one = pair.astype(jnp.float32) + update
    tri_normed = layer_normalized(pair_one, -1).astype(jnp.bfloat16)
    factors = jnp.einsum(
        "ijc,ce->eij",
        tri_normed,
        triangle_input_weight[:, : 4 * pair_chan],
        preferred_element_type=jnp.float32,
    )
    gate_out = jnp.einsum(
        "ijc,ce->ije",
        tri_normed,
        triangle_input_weight[:, 4 * pair_chan :],
        preferred_element_type=jnp.float32,
    )
    left_f = (jax.nn.sigmoid(factors[pair_chan : 2 * pair_chan]) * factors[:pair_chan]).astype(
        jnp.bfloat16
    )
    right_f = (
        jax.nn.sigmoid(factors[3 * pair_chan :]) * factors[2 * pair_chan : 3 * pair_chan]
    ).astype(jnp.bfloat16)
    left_f = left_f.reshape(residue_count, owner_chan, res_local, chain_total)
    right_f = right_f.reshape(residue_count, owner_chan, res_local, chain_total)
    combined = jnp.einsum(
        "xcik,xcjk->xcij",
        lax.all_to_all(left_f, "res", split_axis=0, concat_axis=2, tiled=True),
        lax.all_to_all(right_f, "res", split_axis=0, concat_axis=2, tiled=True),
        preferred_element_type=jnp.float32,
    ).astype(jnp.bfloat16)
    back_rows = lax.all_to_all(combined, "res", split_axis=2, concat_axis=0, tiled=True)
    back_rows = back_rows.reshape(pair_chan, res_local, chain_total)
    comb_normed = layer_normalized(back_rows.astype(jnp.float32), 0).astype(jnp.bfloat16)
    tri_update = jnp.einsum(
        "cij,cz->ijz", comb_normed, triangle_output_weight, preferred_element_type=jnp.float32
    )
    pair_output = (pair_one + jax.nn.sigmoid(gate_out) * tri_update).astype(jnp.bfloat16)
    return (alignment_output, pair_output)


def solution(mesh):
    placed = (
        P(("crop", "res"), None),
        P("crop"),
        P(("crop", "res"), None, None),
        P(("crop", "res"), None, None),
        P(),
        P(),
        P(),
        P(),
        P(),
        P(),
        P(),
        P(),
        P(),
        P(),
    )
    return jax.shard_map(
        shards,
        mesh=mesh,
        in_specs=placed,
        out_specs=(P("crop", "res", None), P(("crop", "res"), None, None)),
        check_vma=False,
    )
```

profile of v0, /device:TPU:0, one launch (start us, length us, event | category | flops | bytes accessed | tf_op | source)
XLA Modules:
  0.0 155.3 jit_solution(11216174859262117624)
XLA Ops:
  0.7 0.7 add_multiply_fusion
  1.4 1.0 copy.74
  2.5 0.8 fusion.14
  3.4 43.9 %all_gather.6 = bf16[8,128,128]{2,0,1:T(8,128)(2,1)S(1)} all-gather(bf16[8,4,128]{2,0,1:T(8,128)(2,1)S(1)} %fusion.14), channel_id=1, replica_groups=mesh['crop'=1,'res'=32] {'res'}, dimensions={1}, use_global_device_ids=true | all-gather | bytes 270336 | tf_op jit(solution)/shard_map/all_gather | solution.py:94
  47.3 0.2 copy.76
  47.6 0.3 fusion.84
  47.9 0.2 multiply_reduce_fusion.3
  48.1 0.3 fusion.85
  48.5 0.7 fusion.83
  49.2 0.1 copy.73
  49.3 0.1 copy.72
  49.5 0.5 copy-done.1
  49.9 0.2 copy-done.2
  50.1 0.5 fusion.86
  50.6 1.3 convolution_add_fusion
  51.9 1.0 copy.71
  53.0 1.0 fusion.20
  54.0 1.1 copy.78
  55.2 1.1 fusion.11
  56.3 0.1 copy.79
  56.4 9.9 %all_to_all.48 = bf16[2,128,256]{2,0,1:T(2,128)(2,1)S(1)} all-to-all(bf16[2,128,256]{2,0,1:T(2,128)(2,1)S(1)} %copy.79), channel_id=1, replica_groups=mesh['crop'=1,'res'=32] {'res'}, dimensions={1} | all-to-all | bytes 262144 | tf_op jit(solution)/shard_map/all_to_all | solution.py:100
  66.4 0.2 reshape.167
  66.6 0.1 bitcast_reduce_fusion.1
  66.7 0.2 multiply_reduce_fusion.2
  66.9 0.3 fusion.87
  67.3 0.7 fusion.82
  68.0 0.2 copy.83
  68.2 0.2 copy.82
  68.4 0.5 fusion.88
  68.9 0.3 fusion.90
  69.2 1.1 copy.81
  70.3 1.2 fusion.19
  71.4 1.2 copy.85
  72.7 1.1 fusion.46
  73.8 0.1 fusion.81
  73.9 0.2 multiply_reduce_fusion.1
  74.1 0.3 convolution_convert_fusion.1
  74.4 0.1 copy.86
  74.5 0.1 reshape.173
  74.7 39.3 %all-gather = bf16[32,4,2048]{2,1,0:T(4,128)(2,1)S(1)} all-gather(bf16[1,4,2048]{2,1,0:T(4,128)(2,1)S(1)} %reshape.173), channel_id=1, replica_groups=mesh['crop'=1,'res'=32] {'res'}, dimensions={0}, use_global_device_ids=true | all-gather | bytes 540672 | tf_op jit(solution)/shard_map/all_gather | solution.py:122
  114.0 1.2 reshape.160
  115.2 2.6 %copy.109 = bf16[128,64,32,1]{0,1,3,2:T(8,128)(2,1)S(1)} copy(bf16[128,64,32,1]{2,1,0,3:T(8,128)(2,1)S(1)} %bitcast.133) | data formatting | bytes 1048576 | tf_op jit(solution)/shard_map/reshape | solution.py:124
  117.8 0.4 fusion.6
  118.2 0.7 copy.88
  118.9 0.4 fusion.89
  119.4 0.3 convolution_bitcast_fusion
  119.7 0.1 fusion.25
  119.8 0.1 copy.97
  120.0 0.7 copy.98
  120.7 2.6 %all-to-all-start.2 = ((bf16[32,4,4,128]{3,1,2,0:T(4,128)(2,1)}), bf16[32,4,4,128]{3,1,2,0:T(4,128)(2,1)S(1)}, u32[]{:S(2)}, u32[]{:S(2)}) async-start(bf16[32,4,4,128]{3,1,2,0:T(4,128)(2,1)} %copy.98), calls=%async_computation.2 | async-start | bytes 262144 | tf_op jit(solution)/shard_map/all_to_all | solution.py:160
  123.3 0.1 copy.94
  123.4 0.7 copy.95
  124.1 7.4 %all-to-all-done.2 = bf16[32,4,4,128]{3,1,2,0:T(4,128)(2,1)S(1)} async-done(((bf16[32,4,4,128]{3,1,2,0:T(4,128)(2,1)}), bf16[32,4,4,128]{3,1,2,0:T(4,128)(2,1)S(1)}, u32[]{:S(2)}, u32[]{:S(2)}) %all-to-all-start.2) | async-done | bytes 131104 | tf_op jit(solution)/shard_map/all_to_all | solution.py:160
  131.5 2.6 %all-to-all-start.1 = ((bf16[32,4,4,128]{3,1,2,0:T(4,128)(2,1)}), bf16[32,4,4,128]{3,1,2,0:T(4,128)(2,1)S(1)}, u32[]{:S(2)}, u32[]{:S(2)}) async-start(bf16[32,4,4,128]{3,1,2,0:T(4,128)(2,1)} %copy.95), calls=%async_computation.1 | async-start | bytes 262144 | tf_op jit(solution)/shard_map/all_to_all | solution.py:159
  134.1 8.1 %all-to-all-done.1 = bf16[32,4,4,128]{3,1,2,0:T(4,128)(2,1)S(1)} async-done(((bf16[32,4,4,128]{3,1,2,0:T(4,128)(2,1)}), bf16[32,4,4,128]{3,1,2,0:T(4,128)(2,1)S(1)}, u32[]{:S(2)}, u32[]{:S(2)}) %all-to-all-start.1) | async-done | bytes 131104 | tf_op jit(solution)/shard_map/all_to_all | solution.py:159
  142.3 0.2 fusion.13
  142.5 0.8 copy.100
  143.3 2.6 %all-to-all-start.3 = ((bf16[1,4,128,128]{3,1,0,2:T(4,128)(2,1)}), bf16[1,4,128,128]{3,1,0,2:T(4,128)(2,1)S(1)}, u32[]{:S(2)}, u32[]{:S(2)}) async-start(bf16[1,4,128,128]{3,1,0,2:T(4,128)(2,1)} %copy.100), calls=%async_computation.3 | async-start | bytes 262144 | tf_op jit(solution)/shard_map/all_to_all | solution.py:163
  145.9 0.8 copy.104
  146.6 0.3 fusion.10
  146.9 7.2 %all-to-all-done.3 = bf16[1,4,128,128]{3,1,0,2:T(4,128)(2,1)S(1)} async-done(((bf16[1,4,128,128]{3,1,0,2:T(4,128)(2,1)}), bf16[1,4,128,128]{3,1,0,2:T(4,128)(2,1)S(1)}, u32[]{:S(2)}, u32[]{:S(2)}) %all-to-all-start.3) | async-done | bytes 131104 | tf_op jit(solution)/shard_map/all_to_all | solution.py:163
  154.2 0.1 fusion.44
  154.3 0.2 fusion.12
  154.6 0.8 copy.105
  (44 shorter events, 0.6 us)
Async XLA Ops:
  0.6 47.5 %copy-start = (bf16[256,1024]{1,0:T(8,128)(2,1)S(1)}, bf16[256,1024]{1,0:T(8,128)(2,1)}, u32[]{:S(2)}) copy-start(bf16[256,1024]{1,0:T(8,128)(2,1)} %param.20) | copy-start | bytes 1572868
  0.6 46.9 %copy-start.9 = (bf16[23,256]{1,0:T(8,128)(2,1)S(1)}, bf16[23,256]{1,0:T(8,128)(2,1)}, u32[]{:S(2)}) copy-start(bf16[23,256]{1,0:T(8,128)(2,1)} %param.18) | copy-start | bytes 35332
  0.7 46.9 %copy-start.5 = (bf16[2,128,256]{2,1,0:T(8,128)(2,1)S(1)}, bf16[2,128,256]{2,1,0:T(8,128)(2,1)}, u32[]{:S(2)}) copy-start(bf16[2,128,256]{2,1,0:T(8,128)(2,1)} %param.16) | copy-start | bytes 393220
  0.7 46.9 %copy-start.10 = (s32[2,128]{1,0:T(2,128)S(1)}, s32[2,128]{1,0:T(2,128)}, u32[]{:S(2)}) copy-start(s32[2,128]{1,0:T(2,128)} %param.14) | copy-start | bytes 3076
  49.3 0.6 copy-start.1
  49.5 0.7 copy-start.2
  54.0 12.9 %copy-start.3 = (bf16[256,1024]{1,0:T(8,128)(2,1)S(1)}, bf16[256,1024]{1,0:T(8,128)(2,1)}, u32[]{:S(2)}) copy-start(bf16[256,1024]{1,0:T(8,128)(2,1)} %param.22) | copy-start | bytes 1572868
  71.4 2.7 %copy-start.7 = (bf16[256,64]{0,1:T(8,128)(2,1)S(1)}, bf16[256,64]{0,1:T(8,128)(2,1)}, u32[]{:S(2)}) copy-start(bf16[256,64]{0,1:T(8,128)(2,1)} %param.24) | copy-start | bytes 98308
  117.8 1.1 copy-start.4
  118.2 1.1 copy-start.6
  120.7 10.8 %all-to-all-start.2 = ((bf16[32,4,4,128]{3,1,2,0:T(4,128)(2,1)}), bf16[32,4,4,128]{3,1,2,0:T(4,128)(2,1)S(1)}, u32[]{:S(2)}, u32[]{:S(2)}) async-start(bf16[32,4,4,128]{3,1,2,0:T(4,128)(2,1)} %copy.98), calls=%async_computation.2 | async-start | bytes 262144 | tf_op jit(solution)/shard_map/all_to_all | solution.py:160
  123.4 30.9 %copy-start.8 = (bf16[128,128]{1,0:T(8,128)(2,1)S(1)}, bf16[128,128]{1,0:T(8,128)(2,1)}, u32[]{:S(2)}) copy-start(bf16[128,128]{1,0:T(8,128)(2,1)} %param.27) | copy-start | bytes 98308
  131.5 10.8 %all-to-all-start.1 = ((bf16[32,4,4,128]{3,1,2,0:T(4,128)(2,1)}), bf16[32,4,4,128]{3,1,2,0:T(4,128)(2,1)S(1)}, u32[]{:S(2)}, u32[]{:S(2)}) async-start(bf16[32,4,4,128]{3,1,2,0:T(4,128)(2,1)} %copy.95), calls=%async_computation.1 | async-start | bytes 262144 | tf_op jit(solution)/shard_map/all_to_all | solution.py:159
  143.3 10.8 %all-to-all-start.3 = ((bf16[1,4,128,128]{3,1,0,2:T(4,128)(2,1)}), bf16[1,4,128,128]{3,1,0,2:T(4,128)(2,1)S(1)}, u32[]{:S(2)}, u32[]{:S(2)}) async-start(bf16[1,4,128,128]{3,1,0,2:T(4,128)(2,1)} %copy.100), calls=%async_computation.3 | async-start | bytes 262144 | tf_op jit(solution)/shard_map/all_to_all | solution.py:163
where the time goes:
time: 156 us; the launch traced here: 155 us
  blocking collectives  93.2 us (60%)
  waiting for transfers between devices  22.7 us (15%)
  local copies, waits for them, and re-layouts  17.4 us (11%)
  matrix products  11 us (7%)
  starting transfers between devices  7.73 us (5%)
  other arithmetic  2.2 us (1%)
    all_gather x1, blocking collectives, shards(): bias_all = lax.all_gather(bias_local, 'res', axis=1, tiled=True)  43.9 us
    all_gather x1, blocking collectives, shards(): piece = lax.all_gather(latter_factor, 'res', axis=0, tiled=True)  39.3 us
    all_to_all x1, blocking collectives, shards(): lax.all_to_all(alignment_after_rows, 'res', split_axis=1, concat_axis=0,...  9.91 us
    all_to_all x1, waiting for transfers between devices, shards(): lax.all_to_all(left_f, 'res', split_axis=0, concat_axis=2, tiled=True)  8.14 us
    all_to_all x1, waiting for transfers between devices, shards(): lax.all_to_all(right_f, 'res', split_axis=0, concat_axis=2, tiled=True)  7.35 us
    all_to_all x1, waiting for transfers between devices, shards(): lax.all_to_all(combined, 'res', split_axis=2, concat_axis=0, tiled=True)  7.17 us
    reshape x2, local copies, waits for them, and re-layouts, shards(): right_rows = piece.reshape(count, sequence_total, outer_chan)  3.78 us
    unnamed x26, local copies, waits for them, and re-layouts  3.38 us
  transfers between devices with their start and end apart: 3, of which 3 were waited for; matrix products, arithmetic and copies ran while one was open for 1% of the time, Pallas kernels for 0%

commit v1 on v0

--- a/solution.py
+++ b/solution.py
@@ -4,6 +4,18 @@
 from jax.sharding import PartitionSpec as P
 
 EPSILON = 1e-05
+
+
+def _link_racks(mesh_dim, where_dim, body):
+    return jnp.concatenate(
+        jax.lax.all_to_all(
+            jnp.stack([body for _ in range(jax.lax.axis_size(mesh_dim))], axis=0),
+            axis_name=mesh_dim,
+            split_axis=0,
+            concat_axis=0,
+        ),
+        axis=where_dim,
+    )
 
 
 def layer_normalized(input_rows, axis):
@@ -119,7 +131,7 @@
         .astype(jnp.bfloat16)
         .reshape(res_local, sequence_total * outer_chan)
     )
-    piece = lax.all_gather(latter_factor, "res", axis=0, tiled=True)
+    piece = _link_racks("res", 0, latter_factor)
     count = piece.shape[0]
     right_rows = piece.reshape(count, sequence_total, outer_chan)
     cross_product_result = (

time: 156 us -> 134 us (0.86)
  blocking collectives: 93.2 us -> 71.2 us
    all_gather x1 -> x0, blocking collectives: 39.3 us -> none  [shards(): piece = lax.all_gather(latter_factor, 'res', axis=0, tiled=True)]
    all_to_all x0 -> x1, blocking collectives: none -> 17.3 us  [_link_racks(): jax.lax.all_to_all(jnp.stack([body for _ in range(jax.lax.axis_size(mesh_...]
    another operation x0 -> x4, local copies, waits for them, and re-layouts: none -> 4.13 us  [the longest x2 3.78 us: shards(): right_rows = piece.reshape(count, sequence_total, outer_chan)]
    reshape x2 -> x0, local copies, waits for them, and re-layouts: 3.78 us -> none  [shards(): right_rows = piece.reshape(count, sequence_total, outer_chan)]
    unnamed x26 -> x25, local copies, waits for them, and re-layouts: 3.38 us -> 3.25 us
where the time goes in v1:
time: 134 us
  blocking collectives  71.2 us (53%)
  waiting for transfers between devices  22.7 us (17%)
  local copies, waits for them, and re-layouts  17.7 us (13%)
  matrix products  11 us (8%)
  starting transfers between devices  8.07 us (6%)
  other arithmetic  2.2 us (2%)
    all_gather x1, blocking collectives, shards(): bias_all = lax.all_gather(bias_local, 'res', axis=1, tiled=True)  43.9 us
    all_to_all x1, blocking collectives, _link_racks(): jax.lax.all_to_all(jnp.stack([body for _ in range(jax.lax.axis_size(mesh_...  17.3 us
    all_to_all x1, blocking collectives, shards(): lax.all_to_all(alignment_after_rows, 'res', split_axis=1, concat_axis=0,...  9.91 us
    all_to_all x1, waiting for transfers between devices, shards(): lax.all_to_all(left_f, 'res', split_axis=0, concat_axis=2, tiled=True)  8.14 us
    all_to_all x1, waiting for transfers between devices, shards(): lax.all_to_all(right_f, 'res', split_axis=0, concat_axis=2, tiled=True)  7.35 us
    all_to_all x1, waiting for transfers between devices, shards(): lax.all_to_all(combined, 'res', split_axis=2, concat_axis=0, tiled=True)  7.17 us
    another operation x2, local copies, waits for them, and re-layouts, shards(): right_rows = piece.reshape(count, sequence_total, outer_chan)  3.78 us
    unnamed x25, local copies, waits for them, and re-layouts  3.25 us
  transfers between devices with their start and end apart: 3, of which 3 were waited for; matrix products, arithmetic and copies ran while one was open for 1% of the time, Pallas kernels for 0%

profile of v1, /device:TPU:0, one launch (start us, length us, event | category | flops | bytes accessed | tf_op | source)
XLA Modules:
  0.0 133.9 jit_solution(4662460981922278406)
XLA Ops:
  0.7 0.7 add_multiply_fusion
  1.4 1.0 copy.74
  2.5 0.8 fusion.14
  3.4 43.9 %all_gather.3 = bf16[8,128,128]{2,0,1:T(8,128)(2,1)S(1)} all-gather(bf16[8,4,128]{2,0,1:T(8,128)(2,1)S(1)} %fusion.14), channel_id=1, replica_groups=mesh['crop'=1,'res'=32] {'res'}, dimensions={1}, use_global_device_ids=true | all-gather | bytes 270336 | tf_op jit(solution)/shard_map/all_gather | solution.py:106
  47.3 0.2 copy.76
  47.6 0.3 fusion.84
  47.9 0.2 multiply_reduce_fusion.3
  48.1 0.3 fusion.85
  48.5 0.7 fusion.83
  49.2 0.1 copy.73
  49.3 0.1 copy.72
  49.5 0.5 copy-done.1
  49.9 0.2 copy-done.2
  50.1 0.5 fusion.86
  50.6 1.3 convolution_add_fusion
  51.9 1.0 copy.71
  53.0 1.0 fusion.20
  54.0 1.1 copy.78
  55.2 1.1 fusion.11
  56.3 0.1 copy.79
  56.4 9.9 %all_to_all.53 = bf16[2,128,256]{2,0,1:T(2,128)(2,1)S(1)} all-to-all(bf16[2,128,256]{2,0,1:T(2,128)(2,1)S(1)} %copy.79), channel_id=1, replica_groups=mesh['crop'=1,'res'=32] {'res'}, dimensions={1} | all-to-all | bytes 262144 | tf_op jit(solution)/shard_map/all_to_all | solution.py:112
  66.4 0.2 reshape.161
  66.6 0.1 bitcast_reduce_fusion.1
  66.7 0.2 multiply_reduce_fusion.2
  66.9 0.3 fusion.87
  67.3 0.7 fusion.82
  68.0 0.2 copy.83
  68.2 0.2 copy.82
  68.4 0.5 fusion.88
  68.9 0.3 fusion.90
  69.2 1.1 copy.81
  70.3 1.2 fusion.19
  71.4 1.2 copy.85
  72.7 1.1 fusion.46
  73.8 0.1 fusion.81
  73.9 0.2 multiply_reduce_fusion.1
  74.1 0.3 convolution_convert_fusion.1
  74.4 0.1 copy.86
  74.5 0.1 stack_reshape.2
  74.7 0.2 stack.3
  74.9 17.3 %all_to_all.54 = bf16[32,4,2048]{2,1,0:T(4,128)(2,1)S(1)} all-to-all(bf16[32,4,2048]{2,1,0:T(4,128)(2,1)S(1)} %stack.3), channel_id=1, replica_groups=mesh['crop'=1,'res'=32] {'res'}, dimensions={0} | all-to-all | bytes 1048576 | tf_op jit(solution)/shard_map/all_to_all | solution.py:11
  92.2 1.2 reshape_reshape.3
  93.4 2.6 %copy.109 = bf16[128,64,32,1]{0,1,3,2:T(8,128)(2,1)S(1)} copy(bf16[128,64,32,1]{2,1,0,3:T(8,128)(2,1)S(1)} %bitcast.133) | data formatting | bytes 1048576 | tf_op jit(solution)/shard_map/reshape;reshape | solution.py:136
  96.0 0.4 fusion.6
  96.5 0.7 copy.88
  97.2 0.4 fusion.89
  97.6 0.3 convolution_bitcast_fusion
  98.0 0.1 fusion.25
  98.1 0.1 copy.97
  98.2 0.7 copy.98
  99.0 2.9 %all-to-all-start.3 = ((bf16[32,4,4,128]{3,1,2,0:T(4,128)(2,1)}), bf16[32,4,4,128]{3,1,2,0:T(4,128)(2,1)S(1)}, u32[]{:S(2)}, u32[]{:S(2)}) async-start(bf16[32,4,4,128]{3,1,2,0:T(4,128)(2,1)} %copy.98), calls=%async_computation.3 | async-start | bytes 262144 | tf_op jit(solution)/shard_map/all_to_all | solution.py:172
  101.9 0.1 copy.94
  102.0 0.7 copy.95
  102.7 7.4 %all-to-all-done.3 = bf16[32,4,4,128]{3,1,2,0:T(4,128)(2,1)S(1)} async-done(((bf16[32,4,4,128]{3,1,2,0:T(4,128)(2,1)}), bf16[32,4,4,128]{3,1,2,0:T(4,128)(2,1)S(1)}, u32[]{:S(2)}, u32[]{:S(2)}) %all-to-all-start.3) | async-done | bytes 131104 | tf_op jit(solution)/shard_map/all_to_all | solution.py:172
  110.1 2.6 %all-to-all-start.2 = ((bf16[32,4,4,128]{3,1,2,0:T(4,128)(2,1)}), bf16[32,4,4,128]{3,1,2,0:T(4,128)(2,1)S(1)}, u32[]{:S(2)}, u32[]{:S(2)}) async-start(bf16[32,4,4,128]{3,1,2,0:T(4,128)(2,1)} %copy.95), calls=%async_computation.2 | async-start | bytes 262144 | tf_op jit(solution)/shard_map/all_to_all | solution.py:171
  112.7 8.1 %all-to-all-done.2 = bf16[32,4,4,128]{3,1,2,0:T(4,128)(2,1)S(1)} async-done(((bf16[32,4,4,128]{3,1,2,0:T(4,128)(2,1)}), bf16[32,4,4,128]{3,1,2,0:T(4,128)(2,1)S(1)}, u32[]{:S(2)}, u32[]{:S(2)}) %all-to-all-start.2) | async-done | bytes 131104 | tf_op jit(solution)/shard_map/all_to_all | solution.py:171
  120.9 0.2 fusion.13
  121.1 0.8 copy.100
  121.9 2.6 %all-to-all-start.4 = ((bf16[1,4,128,128]{3,1,0,2:T(4,128)(2,1)}), bf16[1,4,128,128]{3,1,0,2:T(4,128)(2,1)S(1)}, u32[]{:S(2)}, u32[]{:S(2)}) async-start(bf16[1,4,128,128]{3,1,0,2:T(4,128)(2,1)} %copy.100), calls=%async_computation.4 | async-start | bytes 262144 | tf_op jit(solution)/shard_map/all_to_all | solution.py:175
  124.5 0.8 copy.104
  125.2 0.3 fusion.10
  125.5 7.2 %all-to-all-done.4 = bf16[1,4,128,128]{3,1,0,2:T(4,128)(2,1)S(1)} async-done(((bf16[1,4,128,128]{3,1,0,2:T(4,128)(2,1)}), bf16[1,4,128,128]{3,1,0,2:T(4,128)(2,1)S(1)}, u32[]{:S(2)}, u32[]{:S(2)}) %all-to-all-start.4) | async-done | bytes 131104 | tf_op jit(solution)/shard_map/all_to_all | solution.py:175
  132.9 0.2 fusion.12
  133.2 0.8 copy.105
  (45 shorter events, 0.7 us)
Async XLA Ops:
  0.6 47.5 %copy-start = (bf16[256,1024]{1,0:T(8,128)(2,1)S(1)}, bf16[256,1024]{1,0:T(8,128)(2,1)}, u32[]{:S(2)}) copy-start(bf16[256,1024]{1,0:T(8,128)(2,1)} %param.20) | copy-start | bytes 1572868
  0.6 46.9 %copy-start.9 = (bf16[23,256]{1,0:T(8,128)(2,1)S(1)}, bf16[23,256]{1,0:T(8,128)(2,1)}, u32[]{:S(2)}) copy-start(bf16[23,256]{1,0:T(8,128)(2,1)} %param.18) | copy-start | bytes 35332
  0.7 46.9 %copy-start.5 = (bf16[2,128,256]{2,1,0:T(8,128)(2,1)S(1)}, bf16[2,128,256]{2,1,0:T(8,128)(2,1)}, u32[]{:S(2)}) copy-start(bf16[2,128,256]{2,1,0:T(8,128)(2,1)} %param.16) | copy-start | bytes 393220
  0.7 46.9 %copy-start.10 = (s32[2,128]{1,0:T(2,128)S(1)}, s32[2,128]{1,0:T(2,128)}, u32[]{:S(2)}) copy-start(s32[2,128]{1,0:T(2,128)} %param.14) | copy-start | bytes 3076
  49.3 0.6 copy-start.1
  49.5 0.7 copy-start.2
  54.0 12.9 %copy-start.3 = (bf16[256,1024]{1,0:T(8,128)(2,1)S(1)}, bf16[256,1024]{1,0:T(8,128)(2,1)}, u32[]{:S(2)}) copy-start(bf16[256,1024]{1,0:T(8,128)(2,1)} %param.22) | copy-start | bytes 1572868
  71.4 2.7 %copy-start.7 = (bf16[256,64]{0,1:T(8,128)(2,1)S(1)}, bf16[256,64]{0,1:T(8,128)(2,1)}, u32[]{:S(2)}) copy-start(bf16[256,64]{0,1:T(8,128)(2,1)} %param.24) | copy-start | bytes 98308
  96.0 1.1 copy-start.4
  96.5 1.1 copy-start.6
  99.0 11.1 %all-to-all-start.3 = ((bf16[32,4,4,128]{3,1,2,0:T(4,128)(2,1)}), bf16[32,4,4,128]{3,1,2,0:T(4,128)(2,1)S(1)}, u32[]{:S(2)}, u32[]{:S(2)}) async-start(bf16[32,4,4,128]{3,1,2,0:T(4,128)(2,1)} %copy.98), calls=%async_computation.3 | async-start | bytes 262144 | tf_op jit(solution)/shard_map/all_to_all | solution.py:172
  102.0 30.9 %copy-start.8 = (bf16[128,128]{1,0:T(8,128)(2,1)S(1)}, bf16[128,128]{1,0:T(8,128)(2,1)}, u32[]{:S(2)}) copy-start(bf16[128,128]{1,0:T(8,128)(2,1)} %param.27) | copy-start | bytes 98308
  110.1 10.8 %all-to-all-start.2 = ((bf16[32,4,4,128]{3,1,2,0:T(4,128)(2,1)}), bf16[32,4,4,128]{3,1,2,0:T(4,128)(2,1)S(1)}, u32[]{:S(2)}, u32[]{:S(2)}) async-start(bf16[32,4,4,128]{3,1,2,0:T(4,128)(2,1)} %copy.95), calls=%async_computation.2 | async-start | bytes 262144 | tf_op jit(solution)/shard_map/all_to_all | solution.py:171
  121.9 10.8 %all-to-all-start.4 = ((bf16[1,4,128,128]{3,1,0,2:T(4,128)(2,1)}), bf16[1,4,128,128]{3,1,0,2:T(4,128)(2,1)S(1)}, u32[]{:S(2)}, u32[]{:S(2)}) async-start(bf16[1,4,128,128]{3,1,0,2:T(4,128)(2,1)} %copy.100), calls=%async_computation.4 | async-start | bytes 262144 | tf_op jit(solution)/shard_map/all_to_all | solution.py:175
